TPU v7x, 128 devices: a whole 4x4x4 slice. The times are simulated.
128 devices in a mesh: group: 8 (over y, core), member: 16 (over z, x).
Axes of the slice: x: 4, y: 4, z: 4, core: 2. Of those that a mesh axis runs over, the one named last changes fastest.
Arguments:
- fine_blocks: float32 [2048, 5, 128, 128], P(('group', 'member')), may hold values from -6 to 6
- neighbours: int32 [2048, 5], P(('group', 'member')), may hold values from 0 to 2047, as said below
- slot_one: int32 [2048, 5], P(('group', 'member')), may hold values from 0 to 4
- pair_one: int32 [2048], P(('group', 'member')), may hold values from 0 to 1023, as said below
- prolong_one: float32 [128, 128], replicated, may hold values from -0.5 to 0.5
- slot_two: int32 [1024, 5], P(('group', 'member')), may hold values from 0 to 4
- pair_two: int32 [1024], P(('group', 'member')), may hold values from 0 to 511, as said below
- prolong_two: float32 [128, 128], replicated, may hold values from -0.5 to 0.5
- diag_inverse: float32 [2048, 128, 128], P(('group', 'member')), may hold values from -0.01953125 to 0.01953125
- right_side: float32 [2048, 128], P(('group', 'member')), may hold values from -96 to 96
- initial_guess: float32 [2048, 128], P(('group', 'member')), may hold values from -6 to 6
Outputs:
- coarse_one: float32 [1024, 5, 128, 128], P(('group', 'member'))
- coarse_two: float32 [512, 5, 128, 128], P(('group', 'member'))
- smoothed: float32 [2048, 128], P(('group', 'member'))
Inputs may be any that keep to these rules, and one draw needn't show every extreme that they name: Entry 0 of a row is the row's own element; the other four are its neighbours on a periodic grid and lie in the rows of the same device or of the devices just before and just after it in group-major order, cyclically. `pair_one`: every first-level coarse row is named by exactly two fine elements. A fine element names a coarse row held by a device of its own group; the rows of one device name at most 2 rows held by any one device, and some device names exactly 2 rows of some device. `pair_two`: every second-level coarse row is named by exactly two first-level rows. A first-level row names a row held by a device with the same member index; the rows of one device name at most 2 rows held by any one device, and some device names exactly 2 rows of some device.
All inputs are finite; a program needn't handle non-finite values.
Results may differ from a plain program's by a relative error of at most 0.0001.
Values sent between devices are 32-bit elements; how exact they have to be, the bound alone decides.
A program may use at most 128 MiB of HBM per device.

v0:
```python
import functools

import jax
import jax.numpy as jnp
from jax import lax
from jax.experimental import pallas as pl
from jax.experimental.pallas import tpu as pltpu
from jax.sharding import PartitionSpec as P

MESH = pl.DeviceIdType.MESH
F32 = jnp.float32
BF16 = jnp.bfloat16
I32 = jnp.int32
damping = 0.7

ROWS = 16
LINKS = 5
BLOCK = 128
MEM = 16
GRP = 8
BAND = BLOCK // MEM


def spl(a):
    hi = a.astype(BF16)
    lo = (a - hi.astype(F32)).astype(BF16)
    return hi, lo


def dot3(a, b):
    d = functools.partial(jnp.dot, preferred_element_type=F32)
    return d(a[0], b[0]) + (d(a[0], b[1]) + d(a[1], b[0]))


def kernel(
    nb_s, s1_s, p1_s, s2_s, p2_s,
    fine_h, pr1_h, pr2_h, dinv_h, rhs_h, ig_h,
    co1_h, co2_h, smo_v,
    fine, pr1, pr2, dinv, rhs, win,
    sb1, rb1, srel, rb2, sby, rby, sum2, st1, st2,
    ptab, mpair, mtwo, mpair_r, mtwo_r, tabv,
    tab_s, mtwo_s, tabx_s, tabr_s,
    lsem, msem, wsem, tsem, ssem1, rsem1, ssem2, rsem2, ssemy, rsemy, osem,
):
    g = lax.axis_index("group")
    m = lax.axis_index("member")
    y, co = g // 2, g % 2
    z, x = m // 4, m % 4
    dev = g * MEM + m
    nxt = (dev + 1) % (GRP * MEM)
    prv = (dev + GRP * MEM - 1) % (GRP * MEM)

    loads = [
        pltpu.make_async_copy(fine_h, fine, lsem.at[0]),
        pltpu.make_async_copy(ig_h, win.at[pl.ds(ROWS, ROWS)], lsem.at[1]),
        pltpu.make_async_copy(rhs_h, rhs, lsem.at[2]),
        pltpu.make_async_copy(pr1_h, pr1, lsem.at[3]),
        pltpu.make_async_copy(pr2_h, pr2, lsem.at[4]),
        pltpu.make_async_copy(dinv_h, dinv, lsem.at[5]),
    ]
    for cp in loads:
        cp.start()

    mpeers = []
    for dz, dx in sorted(
        [(dz, dx) for dz in range(4) for dx in range(4) if (dz, dx) != (0, 0)],
        key=lambda o: min(o[0], 4 - o[0]) + min(o[1], 4 - o[1]),
    ):
        mpeers.append(((z + dz) % 4) * 4 + (x + dx) % 4)
    gpeers = []
    for dy in (1, 3, 2, 0):
        for dc in range(2):
            if (dy, dc) != (0, 0):
                gpeers.append(((y + dy) % 4) * 2 + (co + dc) % 2)

    barrier = pltpu.get_barrier_semaphore()
    for t in mpeers:
        pl.semaphore_signal(barrier, inc=1, device_id=(g, t), device_id_type=MESH)
    for t in gpeers:
        pl.semaphore_signal(barrier, inc=1, device_id=(t, m), device_id_type=MESH)
    for t in (nxt, prv):
        pl.semaphore_signal(barrier, inc=1, device_id=(t // MEM, t % MEM), device_id_type=MESH)

    for e in range(ROWS):
        mpair[pl.ds(e, 1), :] = jnp.full((1, BLOCK), p1_s[e], I32)
    lane = lax.broadcasted_iota(I32, (1, BLOCK), 1)
    own2 = [p2_s[c] // (4 * MEM) for c in range(8)]
    for c in range(8):
        rank = jnp.int32(0)
        for b in range(c):
            rank = rank + jnp.where(own2[b] == own2[c], 1, 0)
        row = jnp.where(lane == 0, p2_s[c], jnp.minimum(rank, 1))
        for k in range(LINKS):
            row = jnp.where(lane == 1 + k, s2_s[c, k], row)
        mtwo[pl.ds(c, 1), :] = row
    for gp in range(GRP):
        a0 = jnp.int32(0)
        a1 = jnp.int32(0)
        for c in reversed(range(8)):
            hit = own2[c] == gp
            a1 = jnp.where(hit, a0, a1)
            a0 = jnp.where(hit, c, a0)
        tabx_s[2 * gp] = a0
        tabx_s[2 * gp + 1] = a1

    pl.semaphore_wait(barrier, MEM - 1 + GRP - 1 + 2)

    def remote(src, dst, ss, rs, dev_id):
        pltpu.make_async_remote_copy(
            src_ref=src, dst_ref=dst, send_sem=ss, recv_sem=rs, device_id=dev_id, device_id_type=MESH
        ).start()

    def local(src, dst, s):
        pltpu.make_async_copy(src, dst, s).start()

    for t in mpeers:
        remote(mpair, mpair_r.at[m], msem.at[0], msem.at[1], (g, t))
    local(mpair, mpair_r.at[m], msem.at[1])
    for t in gpeers:
        remote(mtwo, mtwo_r.at[g], msem.at[2], msem.at[3], (t, m))
    local(mtwo, mtwo_r.at[g], msem.at[3])

    def slotted(s):
        @pl.loop(0, ROWS)
        def _(e):
            acc = jnp.where(s1_s[e, 0] == s, 1.0, 0.0) * fine[e, 0]
            for k in range(1, LINKS):
                acc = acc + jnp.where(s1_s[e, k] == s, 1.0, 0.0) * fine[e, k]
            sb1[s, :, e] = acc.reshape(MEM, BAND, BLOCK)

    def send1(s):
        for t in mpeers:
            remote(
                sb1.at[s, t], rb1[s].at[pl.ds(pl.multiple_of(m * ROWS, ROWS), ROWS)],
                ssem1.at[s], rsem1.at[s], (g, t),
            )
        local(sb1.at[s, m], rb1[s].at[pl.ds(pl.multiple_of(m * ROWS, ROWS), ROWS)], rsem1.at[s])

    def relay(s):
        @pl.loop(0, MEM * 8 // 8)
        def _(i):
            for b in range(8):
                c = i * 8 + b
                srel[s, c] = rb1[s][tab_s[0, 0, c]] + rb1[s][tab_s[1, 0, c]]

    def send2(s):
        for t in mpeers:
            remote(
                srel.at[s, pl.ds(pl.multiple_of(t * 8, 8), 8)], rb2[s].at[m],
                ssem2.at[s], rsem2.at[s], (g, t),
            )
        local(srel.at[s, pl.ds(pl.multiple_of(m * 8, 8), 8)], rb2[s].at[m], rsem2.at[s])

    def sendy(s):
        for gp in range(GRP):
            for j in range(2):
                sby[s, gp, j] = rb2[s][:, tabx_s[2 * gp + j]]
        for t in gpeers:
            remote(sby.at[s, t], rby[s].at[g], ssemy.at[s], rsemy.at[s], (t, m))
        local(sby.at[s, g], rby[s].at[g], rsemy.at[s])

    def addy(s):
        @pl.loop(0, 4)
        def _(q):
            rs, ws = [], []
            for i in range(2):
                code = tabr_s[q * 2 + i]
                src = code // 8
                c = code % 8
                rs.append(rby[s][src, jnp.clip(mtwo_s[src, c, 6], 0, 1)])
                ws.append(mtwo_s[src, c, 1 + s])
            for t in range(LINKS):
                add = jnp.where(ws[0] == t, 1.0, 0.0) * rs[0] + jnp.where(ws[1] == t, 1.0, 0.0) * rs[1]
                if s == 0:
                    sum2[q, t] = add
                else:
                    sum2[q, t] = sum2[q, t] + add

    def wait1(s):
        pltpu.make_async_copy(rb1[s], rb1[s], rsem1.at[s]).wait()

    def wait2(s):
        pltpu.make_async_copy(rb2[s], rb2[s], rsem2.at[s]).wait()

    def waity(s):
        pltpu.make_async_copy(rby[s], rby[s], rsemy.at[s]).wait()

    loads[0].wait()
    slotted(0)
    send1(0)
    slotted(1)
    send1(1)
    loads[1].wait()
    remote(
        win.at[pl.ds(ROWS, ROWS)], win.at[pl.ds(0, ROWS)], wsem.at[0], wsem.at[2],
        (nxt // MEM, nxt % MEM),
    )
    remote(
        win.at[pl.ds(ROWS, ROWS)], win.at[pl.ds(2 * ROWS, ROWS)], wsem.at[1], wsem.at[3],
        (prv // MEM, prv % MEM),
    )
    for s in range(2, LINKS):
        slotted(s)

    pltpu.make_async_copy(mpair_r, mpair_r, msem.at[1]).wait()
    cid = lax.broadcasted_iota(I32, (8, BLOCK), 1) + g * (MEM * 8)
    sub = lax.broadcasted_iota(I32, (8, BLOCK), 0)
    lo = jnp.full((8, BLOCK), 1 << 20, I32)
    hi = jnp.full((8, BLOCK), -1, I32)
    for src in range(MEM):
        for h in range(2):
            hit = mpair_r[src, pl.ds(8 * h, 8), :] == cid
            eid = sub + (src * ROWS + 8 * h)
            lo = jnp.minimum(lo, jnp.where(hit, eid, 1 << 20))
            hi = jnp.maximum(hi, jnp.where(hit, eid, -1))
    for sh in (4, 2, 1):
        lo = jnp.minimum(lo, pltpu.roll(lo, sh, 0))
        hi = jnp.maximum(hi, pltpu.roll(hi, sh, 0))
    tabv[0] = jnp.clip(lo, 0, MEM * ROWS - 1)
    tabv[1] = jnp.clip(hi, 0, MEM * ROWS - 1)
    pltpu.make_async_copy(mtwo_r, mtwo_r, msem.at[3]).wait()
    cp_t = pltpu.make_async_copy(tabv, tab_s, tsem.at[0])
    cp_t.start()
    cp_m = pltpu.make_async_copy(mtwo_r, mtwo_s, tsem.at[1])
    cp_m.start()
    cp_t.wait()
    cp_m.wait()
    qbase = dev * 4

    def scan(i, carry):
        v = mtwo_s[i // 8, i % 8, 0]
        out = []
        for q in range(4):
            p0, p1 = carry[2 * q], carry[2 * q + 1]
            hit = v == qbase + q
            out.append(jnp.where(hit, i, p0))
            out.append(jnp.where(hit, p0, p1))
        return tuple(out)

    found = lax.fori_loop(0, 64, scan, tuple(jnp.int32(0) for _ in range(8)))
    for i in range(8):
        tabr_s[i] = found[i]

    for cp in loads[2:]:
        cp.wait()
    pltpu.make_async_copy(win.at[pl.ds(0, ROWS)], win.at[pl.ds(0, ROWS)], wsem.at[2]).wait()
    pltpu.make_async_copy(win.at[pl.ds(0, ROWS)], win.at[pl.ds(2 * ROWS, ROWS)], wsem.at[3]).wait()
    lanes = lax.broadcasted_iota(I32, (BLOCK, BLOCK), 1)
    total = GRP * MEM * ROWS

    def prod(e, cols):
        acc = jnp.zeros((BLOCK, BLOCK), F32)
        for k in range(LINKS):
            at = nb_s[e, k] - dev * ROWS + ROWS
            at = jnp.where(at < 0, at + total, jnp.where(at >= total, at - total, at))
            at = jnp.clip(at, 0, 3 * ROWS - 1)
            acc = acc + fine[e, k] * win[pl.ds(at, 1), :]
        return jnp.where(lanes == e, jnp.sum(acc, axis=1, keepdims=True), cols)

    cols = lax.fori_loop(0, ROWS, prod, jnp.zeros((BLOCK, BLOCK), F32))
    rhs[...] = rhs[...] - cols.T[:ROWS]

    def smooth(e, cols):
        acc = dinv[e] * rhs[pl.ds(e, 1), :]
        return jnp.where(lanes == e, jnp.sum(acc, axis=1, keepdims=True), cols)

    cols = lax.fori_loop(0, ROWS, smooth, jnp.zeros((BLOCK, BLOCK), F32))
    smo_v[...] = win[pl.ds(ROWS, ROWS), :] + damping * cols.T[:ROWS]

    p1 = pr1[...]
    p1r, p1l = spl(p1), spl(p1.T)
    qm = jnp.dot(p1, pr2[...], preferred_element_type=F32, precision=lax.Precision.HIGHEST)
    for i, a in enumerate((*p1r, *p1l, *spl(qm), *spl(qm.T))):
        ptab[i] = a

    def triple(blk, o):
        right = dot3(spl(blk), (ptab[o], ptab[o + 1]))
        return dot3((ptab[o + 2], ptab[o + 3]), spl(right))

    def coarse(s):
        @pl.loop(0, 2)
        def _(i):
            for b in range(4):
                c = i * 4 + b
                st1[s, c] = triple(rb2[s][:, c].reshape(BLOCK, BLOCK), 0)
        pltpu.make_async_copy(st1.at[s], co1_h.at[:, s], osem.at[s]).start()

    for s in range(LINKS):
        wait1(s)
        relay(s)
        send2(s)
        if s + 2 < LINKS:
            send1(s + 2)
        if s >= 1:
            wait2(s - 1)
            sendy(s - 1)
            coarse(s - 1)
        if s >= 2:
            waity(s - 2)
            addy(s - 2)
    last = LINKS - 1
    wait2(last)
    sendy(last)
    waity(last - 1)
    addy(last - 1)
    coarse(last)
    waity(last)
    addy(last)

    @pl.loop(0, 5)
    def _(i):
        for b in range(4):
            j = i * 4 + b
            st2[j] = triple(sum2[j // 5, j % 5].reshape(BLOCK, BLOCK), 4)

    cp2 = pltpu.make_async_copy(st2, co2_h, osem.at[LINKS])
    cp2.start()
    for s in range(LINKS):
        pltpu.make_async_copy(sb1.at[s, pl.ds(0, MEM - 1)], sb1.at[s, pl.ds(0, MEM - 1)], ssem1.at[s]).wait()
        pltpu.make_async_copy(rb2[s].at[pl.ds(0, MEM - 1)], rb2[s].at[pl.ds(0, MEM - 1)], ssem2.at[s]).wait()
        pltpu.make_async_copy(sby.at[s, pl.ds(0, GRP - 1)], sby.at[s, pl.ds(0, GRP - 1)], ssemy.at[s]).wait()
        pltpu.make_async_copy(st1.at[s], co1_h.at[:, s], osem.at[s]).wait()
    pltpu.make_async_copy(mpair_r.at[pl.ds(0, MEM - 1)], mpair_r.at[pl.ds(0, MEM - 1)], msem.at[0]).wait()
    pltpu.make_async_copy(mtwo_r.at[pl.ds(0, GRP - 1)], mtwo_r.at[pl.ds(0, GRP - 1)], msem.at[2]).wait()
    for i in range(2):
        pltpu.make_async_copy(win.at[pl.ds(0, ROWS)], win.at[pl.ds(0, ROWS)], wsem.at[i]).wait()
    cp2.wait()


def local(
    fine_blocks, neighbours, slot_one, pair_one, prolong_one, slot_two, pair_two, prolong_two,
    diag_inverse, right_side, initial_guess,
):
    smem = pl.BlockSpec(memory_space=pltpu.SMEM)
    hbm = pl.BlockSpec(memory_space=pl.ANY)
    vmem = pl.BlockSpec(memory_space=pltpu.VMEM)
    V, S, D = pltpu.VMEM, pltpu.SMEM, pltpu.SemaphoreType.DMA
    co1, co2, smo = pl.pallas_call(
        kernel,
        name="setup",
        out_shape=(
            jax.ShapeDtypeStruct((8, LINKS, BLOCK, BLOCK), F32),
            jax.ShapeDtypeStruct((4 * LINKS, BLOCK, BLOCK), F32),
            jax.ShapeDtypeStruct((ROWS, BLOCK), F32),
        ),
        in_specs=[smem] * 5 + [hbm] * 6,
        out_specs=(hbm, hbm, vmem),
        scratch_shapes=[
            V((ROWS, LINKS, BLOCK, BLOCK), F32),
            V((BLOCK, BLOCK), F32),
            V((BLOCK, BLOCK), F32),
            V((ROWS, BLOCK, BLOCK), F32),
            V((ROWS, BLOCK), F32),
            V((3 * ROWS, BLOCK), F32),
            V((LINKS, MEM, ROWS, BAND, BLOCK), F32),
            [V((MEM * ROWS, BAND, BLOCK), F32)] * LINKS,
            V((LINKS, MEM * 8, BAND, BLOCK), F32),
            [V((MEM, 8, BAND, BLOCK), F32)] * LINKS,
            V((LINKS, GRP, 2, MEM, BAND, BLOCK), F32),
            [V((GRP, 2, MEM, BAND, BLOCK), F32)] * LINKS,
            V((4, LINKS, MEM, BAND, BLOCK), F32),
            V((LINKS, 8, BLOCK, BLOCK), F32),
            V((4 * LINKS, BLOCK, BLOCK), F32),
            V((8, BLOCK, BLOCK), BF16),
            V((ROWS, BLOCK), I32),
            V((8, BLOCK), I32),
            V((MEM, ROWS, BLOCK), I32),
            V((GRP, 8, BLOCK), I32),
            V((2, 8, BLOCK), I32),
            S((2, 8, BLOCK), I32),
            S((GRP, 8, BLOCK), I32),
            S((2 * GRP,), I32),
            S((8,), I32),
            D((6,)), D((4,)), D((4,)), D((2,)),
            D((LINKS,)), D((LINKS,)), D((LINKS,)), D((LINKS,)), D((LINKS,)), D((LINKS,)),
            D((LINKS + 1,)),
        ],
        compiler_params=pltpu.CompilerParams(
            collective_id=0, has_side_effects=True, vmem_limit_bytes=60 * 1024 * 1024
        ),
    )(
        neighbours, slot_one, pair_one, slot_two, pair_two,
        fine_blocks, prolong_one, prolong_two, diag_inverse, right_side, initial_guess,
    )
    return co1, co2.reshape(4, LINKS, BLOCK, BLOCK), smo


def solution(mesh):
    both = ("group", "member")
    return jax.shard_map(
        local,
        mesh=mesh,
        in_specs=(
            P(both, None, None, None), P(both, None), P(both, None), P(both), P(), P(both, None), P(both), P(),
            P(both, None, None), P(both, None), P(both, None),
        ),
        out_specs=(P(both, None, None, None), P(both, None, None, None), P(both, None)),
        check_vma=False,
    )
```

profile of v0, /device:TPU:13, one launch (start us, length us, event | category | flops | bytes accessed | tf_op | source)
XLA Modules:
  0.0 142.8 jit_solution(16265700300786296821)
XLA Ops:
  0.6 1.4 copy.14.nb_s
  2.0 1.4 copy.15.s1_s
  3.4 134.1 %setup.1 = (f32[8,5,128,128]{3,2,1,0:T(8,128)}, f32[20,128,128]{2,1,0:T(8,128)}, f32[16,128]{1,0:T(8,128)}) custom-call(s32[16,5]{1,0:T(8,128)} %copy.14.nb_s, s32[16,5]{1,0:T(8,128)} %copy.15.s1_s, s32[16]{0:T(128)} %p1_s.1, s32[8,5]{1,0:T(8,128)} %s2_s.1, s32[8]{0:T(128)} %p2_s.1, f32[16,5,128,128]{3,2,1,0:T(8,128)} %fine_h.1, f32[128,128]{1,0:T(8,128)} %pr1_h.1, ...), custom_call_target="tpu_custom_call" | custom-call | tf_op jit(solution)/shard_map/setup/pallas_call | solution.py:338
  137.5 0.0 copy-start
  137.5 0.0 copy-start.1
  137.5 3.6 %copy.19 = f32[8,5,128,128]{3,2,1,0:T(8,128)} copy(f32[8,5,128,128]{3,2,1,0:T(8,128)} %get-tuple-element.12) | data formatting | bytes 5242880
  141.1 0.0 copy-done
  141.1 1.1 copy.20
  142.2 0.0 copy-done.1
  142.2 0.6 copy.21
Async XLA Ops:
  137.5 3.7 %copy-start = (f32[20,128,128]{2,1,0:T(8,128)S(1)}, f32[20,128,128]{2,1,0:T(8,128)}, u32[]{:S(2)}) copy-start(f32[20,128,128]{2,1,0:T(8,128)} %get-tuple-element.7) | copy-start | bytes 3932164
  137.5 4.7 %copy-start.1 = (f32[16,128]{1,0:T(8,128)S(1)}, f32[16,128]{1,0:T(8,128)}, u32[]{:S(2)}) copy-start(f32[16,128]{1,0:T(8,128)} %get-tuple-element.14) | copy-start | bytes 24580
where the time goes:
time: 143 us
  Pallas kernels  134 us (94%)
  local copies, waits for them, and re-layouts  8.02 us (6%)
    pallas_call x1, Pallas kernels, local(): pl.pallas_call(kernel, name='setup', out_shape=(jax.ShapeDtypeStruct((8,...  134 us
    unnamed x9, local copies, waits for them, and re-layouts  8.02 us

commit v1 on v0

--- a/solution.py
+++ b/solution.py
@@ -19,6 +19,7 @@
 MEM = 16
 GRP = 8
 BAND = BLOCK // MEM
+LIMIT = 60 * 1024 * 1024
 
 
 def spl(a):
@@ -32,15 +33,37 @@
     return d(a[0], b[0]) + (d(a[0], b[1]) + d(a[1], b[0]))
 
 
+def triple(blk, tab):
+    right = dot3(spl(blk), (tab[0], tab[1]))
+    return dot3((tab[2], tab[3]), spl(right))
+
+
+def finish(co1, sum2, qtab, smo, co1_o, co2_o, smo_o, st2, sem):
+    out = [
+        pltpu.make_async_copy(co1, co1_o, sem.at[0]),
+        pltpu.make_async_copy(smo, smo_o, sem.at[1]),
+    ]
+    for cp in out:
+        cp.start()
+    for i in range(5):
+        for b in range(4):
+            j = i * 4 + b
+            st2[j] = triple(sum2[j].reshape(BLOCK, BLOCK), qtab)
+        out.append(pltpu.make_async_copy(st2.at[pl.ds(4 * i, 4)], co2_o.at[pl.ds(4 * i, 4)], sem.at[2 + i]))
+        out[-1].start()
+    for cp in out:
+        cp.wait()
+
+
 def kernel(
     nb_s, s1_s, p1_s, s2_s, p2_s,
     fine_h, pr1_h, pr2_h, dinv_h, rhs_h, ig_h,
-    co1_h, co2_h, smo_v,
+    co1, sum2, qtab, smo_v,
     fine, pr1, pr2, dinv, rhs, win,
-    sb1, rb1, srel, rb2, sby, rby, sum2, st1, st2,
+    sb1, rb1, srel, rb2, sby, rby, blk, cols_v,
     ptab, mpair, mtwo, mpair_r, mtwo_r, tabv,
     tab_s, mtwo_s, tabx_s, tabr_s,
-    lsem, msem, wsem, tsem, ssem1, rsem1, ssem2, rsem2, ssemy, rsemy, osem,
+    lsem, msem, wsem, tsem, ssem1, rsem1, ssem2, rsem2, ssemy, rsemy,
 ):
     g = lax.axis_index("group")
     m = lax.axis_index("member")
@@ -61,12 +84,13 @@
     for cp in loads:
         cp.start()
 
-    mpeers = []
-    for dz, dx in sorted(
-        [(dz, dx) for dz in range(4) for dx in range(4) if (dz, dx) != (0, 0)],
+    order = sorted(
+        [(dz, dx) for dz in range(4) for dx in range(4)],
         key=lambda o: min(o[0], 4 - o[0]) + min(o[1], 4 - o[1]),
-    ):
-        mpeers.append(((z + dz) % 4) * 4 + (x + dx) % 4)
+    )
+    ahead = [((z + dz) % 4) * 4 + (x + dx) % 4 for dz, dx in order]
+    behind = [((z + 4 - dz) % 4) * 4 + (x + 4 - dx) % 4 for dz, dx in order]
+    mpeers = ahead[1:]
     gpeers = []
     for dy in (1, 3, 2, 0):
         for dc in range(2):
@@ -123,9 +147,9 @@
     def slotted(s):
         @pl.loop(0, ROWS)
         def _(e):
-            acc = jnp.where(s1_s[e, 0] == s, 1.0, 0.0) * fine[e, 0]
+            acc = jnp.where(s1_s[0, e] == s, 1.0, 0.0) * fine[e, 0]
             for k in range(1, LINKS):
-                acc = acc + jnp.where(s1_s[e, k] == s, 1.0, 0.0) * fine[e, k]
+                acc = acc + jnp.where(s1_s[k, e] == s, 1.0, 0.0) * fine[e, k]
             sb1[s, :, e] = acc.reshape(MEM, BAND, BLOCK)
 
     def send1(s):
@@ -144,22 +168,28 @@
                 srel[s, c] = rb1[s][tab_s[0, 0, c]] + rb1[s][tab_s[1, 0, c]]
 
     def send2(s):
-        for t in mpeers:
+        local(srel.at[s, pl.ds(pl.multiple_of(m * 8, 8), 8)], rb2[2 * s].at[0], rsem2.at[2 * s])
+        for i in range(1, MEM):
+            h, t = 2 * s + i // 8, ahead[i]
             remote(
-                srel.at[s, pl.ds(pl.multiple_of(t * 8, 8), 8)], rb2[s].at[m],
-                ssem2.at[s], rsem2.at[s], (g, t),
+                srel.at[s, pl.ds(pl.multiple_of(t * 8, 8), 8)], rb2[h].at[i % 8],
+                ssem2.at[s], rsem2.at[h], (g, t),
             )
-        local(srel.at[s, pl.ds(pl.multiple_of(m * 8, 8), 8)], rb2[s].at[m], rsem2.at[s])
-
-    def sendy(s):
+
+    def sendy(s, h):
+        p = 2 * s + h
+        pltpu.make_async_copy(rb2[p], rb2[p], rsem2.at[p]).wait()
         for gp in range(GRP):
             for j in range(2):
-                sby[s, gp, j] = rb2[s][:, tabx_s[2 * gp + j]]
+                sby[p, gp, j] = rb2[p][:, tabx_s[2 * gp + j]]
         for t in gpeers:
-            remote(sby.at[s, t], rby[s].at[g], ssemy.at[s], rsemy.at[s], (t, m))
-        local(sby.at[s, g], rby[s].at[g], rsemy.at[s])
-
-    def addy(s):
+            remote(sby.at[p, t], rby[p].at[g], ssemy.at[s], rsemy.at[p], (t, m))
+        local(sby.at[p, g], rby[p].at[g], rsemy.at[p])
+
+    def addy(s, h):
+        p = 2 * s + h
+        pltpu.make_async_copy(rby[p], rby[p], rsemy.at[p]).wait()
+
         @pl.loop(0, 4)
         def _(q):
             rs, ws = [], []
@@ -167,23 +197,19 @@
                 code = tabr_s[q * 2 + i]
                 src = code // 8
                 c = code % 8
-                rs.append(rby[s][src, jnp.clip(mtwo_s[src, c, 6], 0, 1)])
+                rs.append(rby[p][src, jnp.clip(mtwo_s[src, c, 6], 0, 1)])
                 ws.append(mtwo_s[src, c, 1 + s])
             for t in range(LINKS):
                 add = jnp.where(ws[0] == t, 1.0, 0.0) * rs[0] + jnp.where(ws[1] == t, 1.0, 0.0) * rs[1]
-                if s == 0:
-                    sum2[q, t] = add
-                else:
-                    sum2[q, t] = sum2[q, t] + add
+                for i in range(8):
+                    b = behind[8 * h + i]
+                    if s == 0:
+                        sum2[q * LINKS + t, b] = add[i]
+                    else:
+                        sum2[q * LINKS + t, b] = sum2[q * LINKS + t, b] + add[i]
 
     def wait1(s):
         pltpu.make_async_copy(rb1[s], rb1[s], rsem1.at[s]).wait()
-
-    def wait2(s):
-        pltpu.make_async_copy(rb2[s], rb2[s], rsem2.at[s]).wait()
-
-    def waity(s):
-        pltpu.make_async_copy(rby[s], rby[s], rsemy.at[s]).wait()
 
     loads[0].wait()
     slotted(0)
@@ -199,8 +225,7 @@
         win.at[pl.ds(ROWS, ROWS)], win.at[pl.ds(2 * ROWS, ROWS)], wsem.at[1], wsem.at[3],
         (prv // MEM, prv % MEM),
     )
-    for s in range(2, LINKS):
-        slotted(s)
+    slotted(2)
 
     pltpu.make_async_copy(mpair_r, mpair_r, msem.at[1]).wait()
     cid = lax.broadcasted_iota(I32, (8, BLOCK), 1) + g * (MEM * 8)
@@ -241,90 +266,102 @@
     for i in range(8):
         tabr_s[i] = found[i]
 
-    for cp in loads[2:]:
-        cp.wait()
-    pltpu.make_async_copy(win.at[pl.ds(0, ROWS)], win.at[pl.ds(0, ROWS)], wsem.at[2]).wait()
-    pltpu.make_async_copy(win.at[pl.ds(0, ROWS)], win.at[pl.ds(2 * ROWS, ROWS)], wsem.at[3]).wait()
     lanes = lax.broadcasted_iota(I32, (BLOCK, BLOCK), 1)
     total = GRP * MEM * ROWS
 
     def prod(e, cols):
         acc = jnp.zeros((BLOCK, BLOCK), F32)
         for k in range(LINKS):
-            at = nb_s[e, k] - dev * ROWS + ROWS
+            at = nb_s[k, e] - dev * ROWS + ROWS
             at = jnp.where(at < 0, at + total, jnp.where(at >= total, at - total, at))
             at = jnp.clip(at, 0, 3 * ROWS - 1)
             acc = acc + fine[e, k] * win[pl.ds(at, 1), :]
         return jnp.where(lanes == e, jnp.sum(acc, axis=1, keepdims=True), cols)
 
-    cols = lax.fori_loop(0, ROWS, prod, jnp.zeros((BLOCK, BLOCK), F32))
-    rhs[...] = rhs[...] - cols.T[:ROWS]
-
     def smooth(e, cols):
         acc = dinv[e] * rhs[pl.ds(e, 1), :]
         return jnp.where(lanes == e, jnp.sum(acc, axis=1, keepdims=True), cols)
 
-    cols = lax.fori_loop(0, ROWS, smooth, jnp.zeros((BLOCK, BLOCK), F32))
-    smo_v[...] = win[pl.ds(ROWS, ROWS), :] + damping * cols.T[:ROWS]
-
-    p1 = pr1[...]
-    p1r, p1l = spl(p1), spl(p1.T)
-    qm = jnp.dot(p1, pr2[...], preferred_element_type=F32, precision=lax.Precision.HIGHEST)
-    for i, a in enumerate((*p1r, *p1l, *spl(qm), *spl(qm.T))):
-        ptab[i] = a
-
-    def triple(blk, o):
-        right = dot3(spl(blk), (ptab[o], ptab[o + 1]))
-        return dot3((ptab[o + 2], ptab[o + 3]), spl(right))
+    def sweep(part):
+        if part == 0:
+            for cp in loads[2:]:
+                cp.wait()
+            pltpu.make_async_copy(win.at[pl.ds(0, ROWS)], win.at[pl.ds(0, ROWS)], wsem.at[2]).wait()
+            pltpu.make_async_copy(win.at[pl.ds(0, ROWS)], win.at[pl.ds(2 * ROWS, ROWS)], wsem.at[3]).wait()
+            cols_v[...] = lax.fori_loop(0, 8, prod, jnp.zeros((BLOCK, BLOCK), F32))
+        elif part == 1:
+            cols = lax.fori_loop(8, ROWS, prod, cols_v[...])
+            rhs[...] = rhs[...] - cols.T[:ROWS]
+        else:
+            cols = lax.fori_loop(0, ROWS, smooth, jnp.zeros((BLOCK, BLOCK), F32))
+            smo_v[...] = win[pl.ds(ROWS, ROWS), :] + damping * cols.T[:ROWS]
+
+    def products():
+        p1 = pr1[...]
+        qm = jnp.dot(p1, pr2[...], preferred_element_type=F32, precision=lax.Precision.HIGHEST)
+        for i, a in enumerate((*spl(p1), *spl(p1.T))):
+            ptab[i] = a
+        for i, a in enumerate((*spl(qm), *spl(qm.T))):
+            qtab[i] = a
 
     def coarse(s):
+        for h in range(2):
+            for i in range(8):
+                blk[:, behind[8 * h + i]] = rb2[2 * s + h][i]
+
         @pl.loop(0, 2)
         def _(i):
             for b in range(4):
                 c = i * 4 + b
-                st1[s, c] = triple(rb2[s][:, c].reshape(BLOCK, BLOCK), 0)
-        pltpu.make_async_copy(st1.at[s], co1_h.at[:, s], osem.at[s]).start()
-
-    for s in range(LINKS):
+                co1[c, s] = triple(blk[c].reshape(BLOCK, BLOCK), ptab)
+
+    def hop(s, then):
         wait1(s)
         relay(s)
         send2(s)
-        if s + 2 < LINKS:
-            send1(s + 2)
-        if s >= 1:
-            wait2(s - 1)
-            sendy(s - 1)
-            coarse(s - 1)
-        if s >= 2:
-            waity(s - 2)
-            addy(s - 2)
-    last = LINKS - 1
-    wait2(last)
-    sendy(last)
-    waity(last - 1)
-    addy(last - 1)
-    coarse(last)
-    waity(last)
-    addy(last)
-
-    @pl.loop(0, 5)
-    def _(i):
-        for b in range(4):
-            j = i * 4 + b
-            st2[j] = triple(sum2[j // 5, j % 5].reshape(BLOCK, BLOCK), 4)
-
-    cp2 = pltpu.make_async_copy(st2, co2_h, osem.at[LINKS])
-    cp2.start()
+        if then is not None:
+            send1(then)
+
+    def up(s):
+        sendy(s, 0)
+        sendy(s, 1)
+        coarse(s)
+
+    def done(s):
+        addy(s, 0)
+        addy(s, 1)
+
+    hop(0, 2)
+    sweep(0)
+    slotted(3)
+    products()
+    hop(1, 3)
+    slotted(4)
+    up(0)
+    sweep(1)
+    hop(2, None)
+    up(1)
+    done(0)
+    sweep(2)
+    hop(3, 4)
+    up(2)
+    done(1)
+    up(3)
+    done(2)
+    hop(4, None)
+    up(4)
+    done(3)
+    done(4)
     for s in range(LINKS):
         pltpu.make_async_copy(sb1.at[s, pl.ds(0, MEM - 1)], sb1.at[s, pl.ds(0, MEM - 1)], ssem1.at[s]).wait()
-        pltpu.make_async_copy(rb2[s].at[pl.ds(0, MEM - 1)], rb2[s].at[pl.ds(0, MEM - 1)], ssem2.at[s]).wait()
-        pltpu.make_async_copy(sby.at[s, pl.ds(0, GRP - 1)], sby.at[s, pl.ds(0, GRP - 1)], ssemy.at[s]).wait()
-        pltpu.make_async_copy(st1.at[s], co1_h.at[:, s], osem.at[s]).wait()
+        pltpu.make_async_copy(srel.at[s, pl.ds(0, 120)], srel.at[s, pl.ds(0, 120)], ssem2.at[s]).wait()
+        pltpu.make_async_copy(
+            sby.at[pl.ds(2 * s, 2), pl.ds(0, GRP - 1)], sby.at[pl.ds(2 * s, 2), pl.ds(0, GRP - 1)], ssemy.at[s]
+        ).wait()
     pltpu.make_async_copy(mpair_r.at[pl.ds(0, MEM - 1)], mpair_r.at[pl.ds(0, MEM - 1)], msem.at[0]).wait()
     pltpu.make_async_copy(mtwo_r.at[pl.ds(0, GRP - 1)], mtwo_r.at[pl.ds(0, GRP - 1)], msem.at[2]).wait()
     for i in range(2):
         pltpu.make_async_copy(win.at[pl.ds(0, ROWS)], win.at[pl.ds(0, ROWS)], wsem.at[i]).wait()
-    cp2.wait()
 
 
 def local(
@@ -332,19 +369,20 @@
     diag_inverse, right_side, initial_guess,
 ):
     smem = pl.BlockSpec(memory_space=pltpu.SMEM)
-    hbm = pl.BlockSpec(memory_space=pl.ANY)
+    hbm = pl.BlockSpec(memory_space=pltpu.HBM)
     vmem = pl.BlockSpec(memory_space=pltpu.VMEM)
     V, S, D = pltpu.VMEM, pltpu.SMEM, pltpu.SemaphoreType.DMA
-    co1, co2, smo = pl.pallas_call(
+    mid = pl.pallas_call(
         kernel,
         name="setup",
         out_shape=(
-            jax.ShapeDtypeStruct((8, LINKS, BLOCK, BLOCK), F32),
-            jax.ShapeDtypeStruct((4 * LINKS, BLOCK, BLOCK), F32),
-            jax.ShapeDtypeStruct((ROWS, BLOCK), F32),
+            V((8, LINKS, BLOCK, BLOCK), F32),
+            V((4 * LINKS, MEM, BAND, BLOCK), F32),
+            V((4, BLOCK, BLOCK), BF16),
+            V((ROWS, BLOCK), F32),
         ),
         in_specs=[smem] * 5 + [hbm] * 6,
-        out_specs=(hbm, hbm, vmem),
+        out_specs=(vmem,) * 4,
         scratch_shapes=[
             V((ROWS, LINKS, BLOCK, BLOCK), F32),
             V((BLOCK, BLOCK), F32),
@@ -355,13 +393,12 @@
             V((LINKS, MEM, ROWS, BAND, BLOCK), F32),
             [V((MEM * ROWS, BAND, BLOCK), F32)] * LINKS,
             V((LINKS, MEM * 8, BAND, BLOCK), F32),
-            [V((MEM, 8, BAND, BLOCK), F32)] * LINKS,
-            V((LINKS, GRP, 2, MEM, BAND, BLOCK), F32),
-            [V((GRP, 2, MEM, BAND, BLOCK), F32)] * LINKS,
-            V((4, LINKS, MEM, BAND, BLOCK), F32),
-            V((LINKS, 8, BLOCK, BLOCK), F32),
-            V((4 * LINKS, BLOCK, BLOCK), F32),
-            V((8, BLOCK, BLOCK), BF16),
+            [V((8, 8, BAND, BLOCK), F32)] * (2 * LINKS),
+            V((2 * LINKS, GRP, 2, 8, BAND, BLOCK), F32),
+            [V((GRP, 2, 8, BAND, BLOCK), F32)] * (2 * LINKS),
+            V((8, MEM, BAND, BLOCK), F32),
+            V((BLOCK, BLOCK), F32),
+            V((4, BLOCK, BLOCK), BF16),
             V((ROWS, BLOCK), I32),
             V((8, BLOCK), I32),
             V((MEM, ROWS, BLOCK), I32),
@@ -372,16 +409,28 @@
             S((2 * GRP,), I32),
             S((8,), I32),
             D((6,)), D((4,)), D((4,)), D((2,)),
-            D((LINKS,)), D((LINKS,)), D((LINKS,)), D((LINKS,)), D((LINKS,)), D((LINKS,)),
-            D((LINKS + 1,)),
+            D((LINKS,)), D((LINKS,)), D((LINKS,)), D((2 * LINKS,)), D((LINKS,)), D((2 * LINKS,)),
         ],
         compiler_params=pltpu.CompilerParams(
-            collective_id=0, has_side_effects=True, vmem_limit_bytes=60 * 1024 * 1024
+            collective_id=0, has_side_effects=True, vmem_limit_bytes=LIMIT
         ),
     )(
-        neighbours, slot_one, pair_one, slot_two, pair_two,
+        neighbours.T, slot_one.T, pair_one, slot_two, pair_two,
         fine_blocks, prolong_one, prolong_two, diag_inverse, right_side, initial_guess,
     )
+    co1, co2, smo = pl.pallas_call(
+        finish,
+        name="finish",
+        out_shape=(
+            jax.ShapeDtypeStruct((8, LINKS, BLOCK, BLOCK), F32),
+            jax.ShapeDtypeStruct((4 * LINKS, BLOCK, BLOCK), F32),
+            jax.ShapeDtypeStruct((ROWS, BLOCK), F32),
+        ),
+        in_specs=[vmem] * 4,
+        out_specs=(hbm,) * 3,
+        scratch_shapes=[V((4 * LINKS, BLOCK, BLOCK), F32), D((7,))],
+        compiler_params=pltpu.CompilerParams(vmem_limit_bytes=16 * 1024 * 1024),
+    )(*mid)
     return co1, co2.reshape(4, LINKS, BLOCK, BLOCK), smo
 
 

time: 143 us -> 117 us (0.82)
  the two profiles are of different devices: /device:TPU:13 before, /device:TPU:1 now
where the time goes in v1:
time: 117 us; the launch traced here: 116 us
  Pallas kernels  116 us (99%)
    pallas_call x1, Pallas kernels, local(): pl.pallas_call(kernel, name='setup', out_shape=(V((8, LINKS, BLOCK, BLOCK...  114 us

profile of v1, /device:TPU:1, one launch (start us, length us, event | category | flops | bytes accessed | tf_op | source)
XLA Modules:
  0.0 116.5 jit_solution(7936478923218153016)
XLA Ops:
  0.6 113.7 %setup.1 = (f32[8,5,128,128]{3,2,1,0:T(8,128)S(1)}, f32[20,16,8,128]{3,2,1,0:T(8,128)S(1)}, bf16[4,128,128]{2,1,0:T(8,128)(2,1)S(1)}, f32[16,128]{1,0:T(8,128)S(1)}) custom-call(s32[5,16]{1,0:T(8,128)} %bitcast.3, s32[5,16]{1,0:T(8,128)} %bitcast.4, s32[16]{0:T(128)} %p1_s.1, s32[8,5]{1,0:T(8,128)} %s2_s.1, s32[8]{0:T(128)} %p2_s.1, ...), custom_call_target="tpu_custom_call" | custom-call | tf_op jit(solution)/shard_map/setup/pallas_call | solution.py:375
  114.4 2.1 %finish.1 = (f32[8,5,128,128]{3,2,1,0:T(8,128)}, f32[20,128,128]{2,1,0:T(8,128)}, f32[16,128]{1,0:T(8,128)}) custom-call(f32[8,5,128,128]{3,2,1,0:T(8,128)S(1)} %get-tuple-element.10.co1, f32[20,16,8,128]{3,2,1,0:T(8,128)S(1)} %get-tuple-element.11.sum2, bf16[4,128,128]{2,1,0:T(8,128)(2,1)S(1)} %get-tuple-element.12.qtab, f32[16,128]{1,0:T(8,128)S(1)} %get-tuple-element.13.smo), custom_call_target="tpu_custom_call" | custom-call | tf_op jit(solution)/shard_map/finish/pallas_call | solution.py:421

commit v2 on v1

--- a/solution.py
+++ b/solution.py
@@ -74,12 +74,15 @@
     prv = (dev + GRP * MEM - 1) % (GRP * MEM)
 
     loads = [
-        pltpu.make_async_copy(fine_h, fine, lsem.at[0]),
-        pltpu.make_async_copy(ig_h, win.at[pl.ds(ROWS, ROWS)], lsem.at[1]),
-        pltpu.make_async_copy(rhs_h, rhs, lsem.at[2]),
-        pltpu.make_async_copy(pr1_h, pr1, lsem.at[3]),
-        pltpu.make_async_copy(pr2_h, pr2, lsem.at[4]),
-        pltpu.make_async_copy(dinv_h, dinv, lsem.at[5]),
+        *[
+            pltpu.make_async_copy(fine_h.at[pl.ds(4 * i, 4)], fine.at[pl.ds(4 * i, 4)], lsem.at[5 + i])
+            for i in range(4)
+        ],
+        pltpu.make_async_copy(ig_h, win.at[pl.ds(ROWS, ROWS)], lsem.at[0]),
+        pltpu.make_async_copy(rhs_h, rhs, lsem.at[1]),
+        pltpu.make_async_copy(pr1_h, pr1, lsem.at[2]),
+        pltpu.make_async_copy(pr2_h, pr2, lsem.at[3]),
+        pltpu.make_async_copy(dinv_h, dinv, lsem.at[4]),
     ]
     for cp in loads:
         cp.start()
@@ -127,67 +130,65 @@
         tabx_s[2 * gp] = a0
         tabx_s[2 * gp + 1] = a1
 
-    pl.semaphore_wait(barrier, MEM - 1 + GRP - 1 + 2)
-
-    def remote(src, dst, ss, rs, dev_id):
-        pltpu.make_async_remote_copy(
-            src_ref=src, dst_ref=dst, send_sem=ss, recv_sem=rs, device_id=dev_id, device_id_type=MESH
-        ).start()
-
-    def local(src, dst, s):
-        pltpu.make_async_copy(src, dst, s).start()
-
-    for t in mpeers:
-        remote(mpair, mpair_r.at[m], msem.at[0], msem.at[1], (g, t))
-    local(mpair, mpair_r.at[m], msem.at[1])
-    for t in gpeers:
-        remote(mtwo, mtwo_r.at[g], msem.at[2], msem.at[3], (t, m))
-    local(mtwo, mtwo_r.at[g], msem.at[3])
-
-    def slotted(s):
-        @pl.loop(0, ROWS)
+    def slotted(s, first=0, count=ROWS):
+        @pl.loop(first, first + count)
         def _(e):
             acc = jnp.where(s1_s[0, e] == s, 1.0, 0.0) * fine[e, 0]
             for k in range(1, LINKS):
                 acc = acc + jnp.where(s1_s[k, e] == s, 1.0, 0.0) * fine[e, k]
             sb1[s, :, e] = acc.reshape(MEM, BAND, BLOCK)
 
+    for i in range(4):
+        loads[i].wait()
+        slotted(0, 4 * i, 4)
+    pl.semaphore_wait(barrier, MEM - 1 + GRP - 1 + 2)
+
+    def remote(src, dst, ss, rs, dev_id):
+        pltpu.make_async_remote_copy(
+            src_ref=src, dst_ref=dst, send_sem=ss, recv_sem=rs, device_id=dev_id, device_id_type=MESH
+        ).start()
+
+    def local(src, dst, s):
+        pltpu.make_async_copy(src, dst, s).start()
+
     def send1(s):
-        for t in mpeers:
-            remote(
-                sb1.at[s, t], rb1[s].at[pl.ds(pl.multiple_of(m * ROWS, ROWS), ROWS)],
-                ssem1.at[s], rsem1.at[s], (g, t),
-            )
-        local(sb1.at[s, m], rb1[s].at[pl.ds(pl.multiple_of(m * ROWS, ROWS), ROWS)], rsem1.at[s])
+        for half in range(2):
+            part = pl.ds(8 * half, 8)
+            spot = pl.ds(pl.multiple_of(m * ROWS + 8 * half, 8), 8)
+            for t in mpeers:
+                remote(sb1.at[s, t, part], rb1[s].at[spot], ssem1.at[s], rsem1.at[s], (g, t))
+        whole = pl.ds(pl.multiple_of(m * ROWS, ROWS), ROWS)
+        local(sb1.at[s, m], rb1[s].at[whole], rsem1.at[s])
 
     def relay(s):
-        @pl.loop(0, MEM * 8 // 8)
-        def _(i):
+        def out(i):
+            p, t = 4 * s + i // 4, ahead[i]
+            src = srel.at[s, pl.ds(pl.multiple_of(t * 8, 8), 8)]
+            if i == 0:
+                local(src, rb2[p].at[0], rsem2.at[p])
+            else:
+                remote(src, rb2[p].at[i % 4], ssem2.at[s], rsem2.at[p], (g, t))
+
+        for i in range(MEM):
             for b in range(8):
-                c = i * 8 + b
+                c = ahead[i] * 8 + b
                 srel[s, c] = rb1[s][tab_s[0, 0, c]] + rb1[s][tab_s[1, 0, c]]
-
-    def send2(s):
-        local(srel.at[s, pl.ds(pl.multiple_of(m * 8, 8), 8)], rb2[2 * s].at[0], rsem2.at[2 * s])
-        for i in range(1, MEM):
-            h, t = 2 * s + i // 8, ahead[i]
-            remote(
-                srel.at[s, pl.ds(pl.multiple_of(t * 8, 8), 8)], rb2[h].at[i % 8],
-                ssem2.at[s], rsem2.at[h], (g, t),
-            )
-
-    def sendy(s, h):
-        p = 2 * s + h
+            if i >= 1:
+                out(i - 1)
+        out(MEM - 1)
+
+    def sendy(p):
         pltpu.make_async_copy(rb2[p], rb2[p], rsem2.at[p]).wait()
-        for gp in range(GRP):
+        for i, t in enumerate((*gpeers, g)):
             for j in range(2):
-                sby[p, gp, j] = rb2[p][:, tabx_s[2 * gp + j]]
-        for t in gpeers:
-            remote(sby.at[p, t], rby[p].at[g], ssemy.at[s], rsemy.at[p], (t, m))
+                sby[p, t, j] = rb2[p][:, tabx_s[2 * t + j]]
+            if i >= 1:
+                to = gpeers[i - 1]
+                remote(sby.at[p, to], rby[p].at[g], ssemy.at[p // 4], rsemy.at[p], (to, m))
         local(sby.at[p, g], rby[p].at[g], rsemy.at[p])
 
-    def addy(s, h):
-        p = 2 * s + h
+    def addy(p):
+        s = p // 4
         pltpu.make_async_copy(rby[p], rby[p], rsemy.at[p]).wait()
 
         @pl.loop(0, 4)
@@ -201,8 +202,8 @@
                 ws.append(mtwo_s[src, c, 1 + s])
             for t in range(LINKS):
                 add = jnp.where(ws[0] == t, 1.0, 0.0) * rs[0] + jnp.where(ws[1] == t, 1.0, 0.0) * rs[1]
-                for i in range(8):
-                    b = behind[8 * h + i]
+                for i in range(4):
+                    b = behind[4 * (p % 4) + i]
                     if s == 0:
                         sum2[q * LINKS + t, b] = add[i]
                     else:
@@ -211,12 +212,17 @@
     def wait1(s):
         pltpu.make_async_copy(rb1[s], rb1[s], rsem1.at[s]).wait()
 
-    loads[0].wait()
-    slotted(0)
     send1(0)
+    for t in mpeers:
+        remote(mpair, mpair_r.at[m], msem.at[0], msem.at[1], (g, t))
+    local(mpair, mpair_r.at[m], msem.at[1])
+    for t in gpeers:
+        remote(mtwo, mtwo_r.at[g], msem.at[2], msem.at[3], (t, m))
+    local(mtwo, mtwo_r.at[g], msem.at[3])
+
     slotted(1)
     send1(1)
-    loads[1].wait()
+    loads[4].wait()
     remote(
         win.at[pl.ds(ROWS, ROWS)], win.at[pl.ds(0, ROWS)], wsem.at[0], wsem.at[2],
         (nxt // MEM, nxt % MEM),
@@ -284,7 +290,7 @@
 
     def sweep(part):
         if part == 0:
-            for cp in loads[2:]:
+            for cp in loads[5:]:
                 cp.wait()
             pltpu.make_async_copy(win.at[pl.ds(0, ROWS)], win.at[pl.ds(0, ROWS)], wsem.at[2]).wait()
             pltpu.make_async_copy(win.at[pl.ds(0, ROWS)], win.at[pl.ds(2 * ROWS, ROWS)], wsem.at[3]).wait()
@@ -305,9 +311,8 @@
             qtab[i] = a
 
     def coarse(s):
-        for h in range(2):
-            for i in range(8):
-                blk[:, behind[8 * h + i]] = rb2[2 * s + h][i]
+        for i in range(MEM):
+            blk[:, behind[i]] = rb2[4 * s + i // 4][i % 4]
 
         @pl.loop(0, 2)
         def _(i):
@@ -318,18 +323,17 @@
     def hop(s, then):
         wait1(s)
         relay(s)
-        send2(s)
         if then is not None:
             send1(then)
 
     def up(s):
-        sendy(s, 0)
-        sendy(s, 1)
+        for i in range(4):
+            sendy(4 * s + i)
         coarse(s)
 
     def done(s):
-        addy(s, 0)
-        addy(s, 1)
+        for i in range(4):
+            addy(4 * s + i)
 
     hop(0, 2)
     sweep(0)
@@ -356,7 +360,7 @@
         pltpu.make_async_copy(sb1.at[s, pl.ds(0, MEM - 1)], sb1.at[s, pl.ds(0, MEM - 1)], ssem1.at[s]).wait()
         pltpu.make_async_copy(srel.at[s, pl.ds(0, 120)], srel.at[s, pl.ds(0, 120)], ssem2.at[s]).wait()
         pltpu.make_async_copy(
-            sby.at[pl.ds(2 * s, 2), pl.ds(0, GRP - 1)], sby.at[pl.ds(2 * s, 2), pl.ds(0, GRP - 1)], ssemy.at[s]
+            sby.at[pl.ds(4 * s, 4), pl.ds(0, GRP - 1)], sby.at[pl.ds(4 * s, 4), pl.ds(0, GRP - 1)], ssemy.at[s]
         ).wait()
     pltpu.make_async_copy(mpair_r.at[pl.ds(0, MEM - 1)], mpair_r.at[pl.ds(0, MEM - 1)], msem.at[0]).wait()
     pltpu.make_async_copy(mtwo_r.at[pl.ds(0, GRP - 1)], mtwo_r.at[pl.ds(0, GRP - 1)], msem.at[2]).wait()
@@ -393,9 +397,9 @@
             V((LINKS, MEM, ROWS, BAND, BLOCK), F32),
             [V((MEM * ROWS, BAND, BLOCK), F32)] * LINKS,
             V((LINKS, MEM * 8, BAND, BLOCK), F32),
-            [V((8, 8, BAND, BLOCK), F32)] * (2 * LINKS),
-            V((2 * LINKS, GRP, 2, 8, BAND, BLOCK), F32),
-            [V((GRP, 2, 8, BAND, BLOCK), F32)] * (2 * LINKS),
+            [V((4, 8, BAND, BLOCK), F32)] * (4 * LINKS),
+            V((4 * LINKS, GRP, 2, 4, BAND, BLOCK), F32),
+            [V((GRP, 2, 4, BAND, BLOCK), F32)] * (4 * LINKS),
             V((8, MEM, BAND, BLOCK), F32),
             V((BLOCK, BLOCK), F32),
             V((4, BLOCK, BLOCK), BF16),
@@ -408,8 +412,8 @@
             S((GRP, 8, BLOCK), I32),
             S((2 * GRP,), I32),
             S((8,), I32),
-            D((6,)), D((4,)), D((4,)), D((2,)),
-            D((LINKS,)), D((LINKS,)), D((LINKS,)), D((2 * LINKS,)), D((LINKS,)), D((2 * LINKS,)),
+            D((9,)), D((4,)), D((4,)), D((2,)),
+            D((LINKS,)), D((LINKS,)), D((LINKS,)), D((4 * LINKS,)), D((LINKS,)), D((4 * LINKS,)),
         ],
         compiler_params=pltpu.CompilerParams(
             collective_id=0, has_side_effects=True, vmem_limit_bytes=LIMIT

time: 117 us -> 113 us (0.966)
  Pallas kernels: 116 us -> 113 us
    pallas_call x1, Pallas kernels: 114 us -> 110 us  [local(): pl.pallas_call(kernel, name='setup', out_shape=(V((8, LINKS, BLOCK, BLOCK...]
where the time goes in v2:
time: 113 us
  Pallas kernels  113 us (100%)
    pallas_call x1, Pallas kernels, local(): pl.pallas_call(kernel, name='setup', out_shape=(V((8, LINKS, BLOCK, BLOCK...  110 us

profile of v2, /device:TPU:1, one launch (start us, length us, event | category | flops | bytes accessed | tf_op | source)
XLA Modules:
  0.0 113.2 jit_solution(8966831255439777148)
XLA Ops:
  0.6 110.5 %setup.1 = (f32[8,5,128,128]{3,2,1,0:T(8,128)S(1)}, f32[20,16,8,128]{3,2,1,0:T(8,128)S(1)}, bf16[4,128,128]{2,1,0:T(8,128)(2,1)S(1)}, f32[16,128]{1,0:T(8,128)S(1)}) custom-call(s32[5,16]{1,0:T(8,128)} %bitcast.3, s32[5,16]{1,0:T(8,128)} %bitcast.4, s32[16]{0:T(128)} %p1_s.1, s32[8,5]{1,0:T(8,128)} %s2_s.1, s32[8]{0:T(128)} %p2_s.1, ...), custom_call_target="tpu_custom_call" | custom-call | tf_op jit(solution)/shard_map/setup/pallas_call | solution.py:379
  111.1 2.1 %finish.1 = (f32[8,5,128,128]{3,2,1,0:T(8,128)}, f32[20,128,128]{2,1,0:T(8,128)}, f32[16,128]{1,0:T(8,128)}) custom-call(f32[8,5,128,128]{3,2,1,0:T(8,128)S(1)} %get-tuple-element.10.co1, f32[20,16,8,128]{3,2,1,0:T(8,128)S(1)} %get-tuple-element.11.sum2, bf16[4,128,128]{2,1,0:T(8,128)(2,1)S(1)} %get-tuple-element.12.qtab, f32[16,128]{1,0:T(8,128)S(1)} %get-tuple-element.13.smo), custom_call_target="tpu_custom_call" | custom-call | tf_op jit(solution)/shard_map/finish/pallas_call | solution.py:425

commit v3 on v2

--- a/solution.py
+++ b/solution.py
@@ -56,13 +56,13 @@
 
 
 def kernel(
-    nb_s, s1_s, p1_s, s2_s, p2_s,
+    nb_h, s1_h, p1_h, s2_h, p2_h,
     fine_h, pr1_h, pr2_h, dinv_h, rhs_h, ig_h,
     co1, sum2, qtab, smo_v,
     fine, pr1, pr2, dinv, rhs, win,
     sb1, rb1, srel, rb2, sby, rby, blk, cols_v,
     ptab, mpair, mtwo, mpair_r, mtwo_r, tabv,
-    tab_s, mtwo_s, tabx_s, tabr_s,
+    nb_s, s1_s, p1_s, s2_s, p2_s, tab_s, mtwo_s, tabx_s, tabr_s,
     lsem, msem, wsem, tsem, ssem1, rsem1, ssem2, rsem2, ssemy, rsemy,
 ):
     g = lax.axis_index("group")
@@ -84,6 +84,12 @@
         pltpu.make_async_copy(pr2_h, pr2, lsem.at[3]),
         pltpu.make_async_copy(dinv_h, dinv, lsem.at[4]),
     ]
+    ints = [
+        pltpu.make_async_copy(a, b, tsem.at[2 + i])
+        for i, (a, b) in enumerate(((s1_h, s1_s), (p1_h, p1_s), (p2_h, p2_s), (s2_h, s2_s), (nb_h, nb_s)))
+    ]
+    for cp in ints:
+        cp.start()
     for cp in loads:
         cp.start()
 
@@ -108,6 +114,8 @@
     for t in (nxt, prv):
         pl.semaphore_signal(barrier, inc=1, device_id=(t // MEM, t % MEM), device_id_type=MESH)
 
+    for cp in ints:
+        cp.wait()
     for e in range(ROWS):
         mpair[pl.ds(e, 1), :] = jnp.full((1, BLOCK), p1_s[e], I32)
     lane = lax.broadcasted_iota(I32, (1, BLOCK), 1)
@@ -151,14 +159,13 @@
     def local(src, dst, s):
         pltpu.make_async_copy(src, dst, s).start()
 
-    def send1(s):
-        for half in range(2):
-            part = pl.ds(8 * half, 8)
-            spot = pl.ds(pl.multiple_of(m * ROWS + 8 * half, 8), 8)
+    def send1(s, parts=range(4)):
+        for part in parts:
+            rows = pl.ds(4 * part, 4)
+            spot = pl.ds(pl.multiple_of(m * ROWS + 4 * part, 4), 4)
             for t in mpeers:
-                remote(sb1.at[s, t, part], rb1[s].at[spot], ssem1.at[s], rsem1.at[s], (g, t))
-        whole = pl.ds(pl.multiple_of(m * ROWS, ROWS), ROWS)
-        local(sb1.at[s, m], rb1[s].at[whole], rsem1.at[s])
+                remote(sb1.at[s, t, rows], rb1[s].at[spot], ssem1.at[s], rsem1.at[s], (g, t))
+            local(sb1.at[s, m, rows], rb1[s].at[spot], rsem1.at[s])
 
     def relay(s):
         def out(i):
@@ -353,8 +360,10 @@
     up(3)
     done(2)
     hop(4, None)
-    up(4)
-    done(3)
+    for i in range(4):
+        sendy(16 + i)
+        addy(12 + i)
+    coarse(4)
     done(4)
     for s in range(LINKS):
         pltpu.make_async_copy(sb1.at[s, pl.ds(0, MEM - 1)], sb1.at[s, pl.ds(0, MEM - 1)], ssem1.at[s]).wait()
@@ -372,7 +381,6 @@
     fine_blocks, neighbours, slot_one, pair_one, prolong_one, slot_two, pair_two, prolong_two,
     diag_inverse, right_side, initial_guess,
 ):
-    smem = pl.BlockSpec(memory_space=pltpu.SMEM)
     hbm = pl.BlockSpec(memory_space=pltpu.HBM)
     vmem = pl.BlockSpec(memory_space=pltpu.VMEM)
     V, S, D = pltpu.VMEM, pltpu.SMEM, pltpu.SemaphoreType.DMA
@@ -385,7 +393,7 @@
             V((4, BLOCK, BLOCK), BF16),
             V((ROWS, BLOCK), F32),
         ),
-        in_specs=[smem] * 5 + [hbm] * 6,
+        in_specs=[hbm] * 11,
         out_specs=(vmem,) * 4,
         scratch_shapes=[
             V((ROWS, LINKS, BLOCK, BLOCK), F32),
@@ -408,11 +416,12 @@
             V((MEM, ROWS, BLOCK), I32),
             V((GRP, 8, BLOCK), I32),
             V((2, 8, BLOCK), I32),
+            S((LINKS, ROWS), I32), S((LINKS, ROWS), I32), S((ROWS,), I32), S((8, LINKS), I32), S((8,), I32),
             S((2, 8, BLOCK), I32),
             S((GRP, 8, BLOCK), I32),
             S((2 * GRP,), I32),
             S((8,), I32),
-            D((9,)), D((4,)), D((4,)), D((2,)),
+            D((9,)), D((4,)), D((4,)), D((7,)),
             D((LINKS,)), D((LINKS,)), D((LINKS,)), D((4 * LINKS,)), D((LINKS,)), D((4 * LINKS,)),
         ],
         compiler_params=pltpu.CompilerParams(

time: 113 us -> 112 us (level)
  Pallas kernels: 113 us -> 111 us
    pallas_call x1, Pallas kernels: 110 us -> 109 us  [local(): pl.pallas_call(kernel, name='setup', out_shape=(V((8, LINKS, BLOCK, BLOCK...]
where the time goes in v3:
time: 112 us
  Pallas kernels  111 us (99%)
    pallas_call x1, Pallas kernels, local(): pl.pallas_call(kernel, name='setup', out_shape=(V((8, LINKS, BLOCK, BLOCK...  109 us

profile of v3, /device:TPU:1, one launch (start us, length us, event | category | flops | bytes accessed | tf_op | source)
XLA Modules:
  0.0 111.7 jit_solution(15021818335373049142)
XLA Ops:
  0.6 109.0 %setup.1 = (f32[8,5,128,128]{3,2,1,0:T(8,128)S(1)}, f32[20,16,8,128]{3,2,1,0:T(8,128)S(1)}, bf16[4,128,128]{2,1,0:T(8,128)(2,1)S(1)}, f32[16,128]{1,0:T(8,128)S(1)}) custom-call(s32[5,16]{1,0:T(8,128)} %bitcast.3, s32[5,16]{1,0:T(8,128)} %bitcast.4, s32[16]{0:T(128)} %p1_h.1, s32[8,5]{1,0:T(8,128)} %s2_h.1, s32[8]{0:T(128)} %p2_h.1, ...), custom_call_target="tpu_custom_call" | custom-call | tf_op jit(solution)/shard_map/setup/pallas_call | solution.py:387
  109.6 2.1 %finish.1 = (f32[8,5,128,128]{3,2,1,0:T(8,128)}, f32[20,128,128]{2,1,0:T(8,128)}, f32[16,128]{1,0:T(8,128)}) custom-call(f32[8,5,128,128]{3,2,1,0:T(8,128)S(1)} %get-tuple-element.10.co1, f32[20,16,8,128]{3,2,1,0:T(8,128)S(1)} %get-tuple-element.11.sum2, bf16[4,128,128]{2,1,0:T(8,128)(2,1)S(1)} %get-tuple-element.12.qtab, f32[16,128]{1,0:T(8,128)S(1)} %get-tuple-element.13.smo), custom_call_target="tpu_custom_call" | custom-call | tf_op jit(solution)/shard_map/finish/pallas_call | solution.py:434

commit v4 on v3

--- a/solution.py
+++ b/solution.py
@@ -239,6 +239,8 @@
         (prv // MEM, prv % MEM),
     )
     slotted(2)
+    send1(2, (0,))
+    slotted(3)
 
     pltpu.make_async_copy(mpair_r, mpair_r, msem.at[1]).wait()
     cid = lax.broadcasted_iota(I32, (8, BLOCK), 1) + g * (MEM * 8)
@@ -327,11 +329,11 @@
                 c = i * 4 + b
                 co1[c, s] = triple(blk[c].reshape(BLOCK, BLOCK), ptab)
 
-    def hop(s, then):
+    def hop(s, *then):
         wait1(s)
         relay(s)
-        if then is not None:
-            send1(then)
+        for t in then:
+            send1(*t)
 
     def up(s):
         for i in range(4):
@@ -342,24 +344,23 @@
         for i in range(4):
             addy(4 * s + i)
 
-    hop(0, 2)
+    hop(0, (2, (1, 2, 3)), (3, (0,)))
     sweep(0)
-    slotted(3)
     products()
-    hop(1, 3)
+    hop(1, (3, (1, 2, 3)))
     slotted(4)
     up(0)
     sweep(1)
-    hop(2, None)
+    hop(2, (4, (0,)))
     up(1)
     done(0)
     sweep(2)
-    hop(3, 4)
+    hop(3, (4, (1, 2, 3)))
     up(2)
     done(1)
     up(3)
     done(2)
-    hop(4, None)
+    hop(4)
     for i in range(4):
         sendy(16 + i)
         addy(12 + i)

time: 112 us -> 112 us (level)
  no operation moved by 1% of the time
where the time goes in v4:
time: 112 us
  Pallas kernels  111 us (99%)
    pallas_call x1, Pallas kernels, local(): pl.pallas_call(kernel, name='setup', out_shape=(V((8, LINKS, BLOCK, BLOCK...  109 us

profile of v4, /device:TPU:1, one launch (start us, length us, event | category | flops | bytes accessed | tf_op | source)
XLA Modules:
  0.0 111.7 jit_solution(3060785994529123486)
XLA Ops:
  0.6 109.0 %setup.1 = (f32[8,5,128,128]{3,2,1,0:T(8,128)S(1)}, f32[20,16,8,128]{3,2,1,0:T(8,128)S(1)}, bf16[4,128,128]{2,1,0:T(8,128)(2,1)S(1)}, f32[16,128]{1,0:T(8,128)S(1)}) custom-call(s32[5,16]{1,0:T(8,128)} %bitcast.3, s32[5,16]{1,0:T(8,128)} %bitcast.4, s32[16]{0:T(128)} %p1_h.1, s32[8,5]{1,0:T(8,128)} %s2_h.1, s32[8]{0:T(128)} %p2_h.1, ...), custom_call_target="tpu_custom_call" | custom-call | tf_op jit(solution)/shard_map/setup/pallas_call | solution.py:388
  109.6 2.1 %finish.1 = (f32[8,5,128,128]{3,2,1,0:T(8,128)}, f32[20,128,128]{2,1,0:T(8,128)}, f32[16,128]{1,0:T(8,128)}) custom-call(f32[8,5,128,128]{3,2,1,0:T(8,128)S(1)} %get-tuple-element.10.co1, f32[20,16,8,128]{3,2,1,0:T(8,128)S(1)} %get-tuple-element.11.sum2, bf16[4,128,128]{2,1,0:T(8,128)(2,1)S(1)} %get-tuple-element.12.qtab, f32[16,128]{1,0:T(8,128)S(1)} %get-tuple-element.13.smo), custom_call_target="tpu_custom_call" | custom-call | tf_op jit(solution)/shard_map/finish/pallas_call | solution.py:435
